TPU v7x, 32 devices: a whole 2x2x4 slice. The times are simulated.
32 devices in a mesh: grp: 4 (over z), mem: 8 (over y, x, core).
Axes of the slice: x: 2, y: 2, z: 4, core: 2. Of those that a mesh axis runs over, the one named last changes fastest.
Arguments:
- child_means: float32 [65536, 64], P(('grp', 'mem')), may hold values from -48 to 48
- child_variances: float32 [65536, 64], P(('grp', 'mem')), may hold values from 0.2 to 2
- virtual_counts: int32 [65536], P(('grp', 'mem')), may hold values from 1 to 4
- assignment: int32 [65536, 1], P(('grp', 'mem')), may hold values from 0 to 511
Outputs:
- parent_means: float32 [512, 64], P('mem')
- parent_variances: float32 [512, 64], P('mem')
- parent_weights: float32 [512], P('mem')
All inputs are finite; a program needn't handle non-finite values.
Results may differ from a plain program's by a relative error of at most 0.0003.
Values sent between devices are 32-bit elements; how exact they have to be, the bound alone decides.
A program may use at most 64 MiB of HBM per device.

v0:
```python
import math
import jax
import jax.numpy as jnp
from jax import lax
from jax.sharding import PartitionSpec as P

P_SIZE = 512
ITERS = 2


def child_features(means, variances):
    return jnp.concatenate([means, variances + means * means], axis=1)


def accumulate(features, extras, weigh):
    row_count = features.shape[0]
    block = math.gcd(row_count, 1024)
    turns = row_count // block
    pieces = (features.reshape(turns, block, features.shape[1]),) + tuple(
        (extra.reshape((turns, block) + extra.shape[1:]) for extra in extras)
    )

    def advance(carry, piece):
        weights = weigh(*piece)
        sums = carry[0] + lax.dot_general(
            weights,
            piece[0],
            (((0,), (0,)), ((), ())),
            precision=lax.Precision.HIGHEST,
            preferred_element_type=jnp.float32,
        )
        counts = carry[1] + jnp.sum(weights, axis=0)
        return ((sums, counts), None)

    start_sums = (
        jnp.zeros((P_SIZE, features.shape[1]), jnp.float32),
        jnp.zeros((P_SIZE,), jnp.float32),
    )
    return lax.scan(advance, start_sums, pieces)[0]


def maximize(counts, sums, total):
    width = sums.shape[1] // 2
    mass = counts + 1.0
    means = sums[:, :width] / mass[:, None]
    second = (sums[:, width:] + 1.0) / mass[:, None]
    return (means, second - means * means, mass / (total + P_SIZE))


def parent_table(means, variances, weights):
    inverse = 1.0 / variances
    table = jnp.concatenate([-2.0 * means * inverse, inverse], axis=1)
    offset = jnp.sum(jnp.log(2.0 * math.pi * variances) + means * means * inverse, axis=1)
    return (table, offset, jnp.log(weights))


def soft_weights(block_features, block_virtual, table, offset, log_weight):
    width = block_features.shape[1] // 2
    cross = lax.dot_general(
        block_features,
        table,
        (((1,), (1,)), ((), ())),
        precision=lax.Precision.HIGHEST,
        preferred_element_type=jnp.float32,
    )
    ell = -0.5 / width * (cross + offset[None, :])
    score = log_weight[None, :] + block_virtual[:, None] * ell
    top = jnp.max(score, axis=1, keepdims=True)
    expd = jnp.exp(score - top)
    resp = expd / jnp.sum(expd, axis=1, keepdims=True)
    return resp * block_virtual[:, None]


def shards(child_means, child_variances, virtual_counts, assignment):
    features = child_features(child_means, child_variances)
    virtual = virtual_counts.astype(jnp.float32)
    labels = jnp.arange(P_SIZE, dtype=jnp.int32)

    def initial_weights(block_features, block_virtual, block_assign):
        return (block_assign == labels[None, :]).astype(jnp.float32) * block_virtual[:, None]

    sums, counts = accumulate(features, (virtual, assignment), initial_weights)
    total = lax.psum(jnp.sum(virtual), ("grp", "mem"))

    def combine(local_sums, local_counts):
        shared = (
            lax.psum_scatter(local_sums, "mem", scatter_dimension=0, tiled=True),
            lax.psum_scatter(local_counts, "mem", scatter_dimension=0, tiled=True),
        )
        return lax.psum((shared[0], shared[1]), "grp")

    own_sums, own_counts = combine(sums, counts)
    means, variances, weights = maximize(own_counts, own_sums, total)
    for iteration in range(ITERS):
        all_means, all_variances, all_weights = (
            lax.all_gather(means, "mem", axis=0, tiled=True),
            lax.all_gather(variances, "mem", axis=0, tiled=True),
            lax.all_gather(weights, "mem", axis=0, tiled=True),
        )
        table, offset, log_weight = parent_table(all_means, all_variances, all_weights)

        def weigh(block_features, block_virtual):
            return soft_weights(block_features, block_virtual, table, offset, log_weight)

        sums, counts = accumulate(features, (virtual,), weigh)
        own_sums, own_counts = combine(sums, counts)
        means, variances, weights = maximize(own_counts, own_sums, total)
    return (means, variances, weights)


def solution(mesh):
    in_specs = (
        P(("grp", "mem"), None),
        P(("grp", "mem"), None),
        P(("grp", "mem")),
        P(("grp", "mem"), None),
    )
    out_specs = (P("mem", None), P("mem", None), P("mem"))
    return jax.shard_map(shards, mesh=mesh, in_specs=in_specs, out_specs=out_specs, check_vma=False)
```

profile of v0, /device:TPU:0, one launch (start us, length us, event | category | flops | bytes accessed | tf_op | source)
XLA Modules:
  0.0 293.5 jit_solution(11252077472539837460)
XLA Ops:
  7.2 0.0 reduce-scatter.4.cloned.1.call-start
  7.2 1.3 multiply_add_fusion.2
  8.5 1.2 pad_maximum_fusion
  9.7 0.3 copy.9
  10.1 8.4 %while.39 = (s32[]{:T(128)}, f32[512,128]{1,0:T(8,128)S(1)}, f32[512]{0:T(512)S(1)}, s32[2,1024,1]{1,2,0:T(1,128)S(1)}, f32[2,1024]{1,0:T(2,128)S(1)}, /*index=5*/f32[2,1024,128]{2,1,0:T(8,128)S(1)}, s32[]{:T(128)}, s32[]{:T(128)}) while((s32[]{:T(128)}, f32[512,128]{1,0:T(8,128)S(1)}, f32[512]{0:T(512)S(1)}, ...), condition=%wide.region_2.3_spmd.clone, body=%wide.region_0.2_spmd.clone.sunk | while | flops 808059392 | bytes 1089644 | solution.py:39
  10.1 3.8 %fusion.56 = f32[512,128]{1,0:T(8,128)S(1)} fusion(f32[1024]{0:T(1024)S(1)} %bitcast.56, s32[1024]{0:T(1024)S(1)} %bitcast.58, f32[2,1024,128]{2,1,0:T(8,128)S(1)} %get-tuple-element.448, s32[]{:T(128)} %get-tuple-element.435, f32[512,128]{1,0:T(8,128)S(1)} %get-tuple-element.436, pred[]{:T(512)S(6)} %compare.9), kind=kOutput, calls=%fused_computation.5.clone.1 | convolution fusion | flops 806486016 | bytes 1056773 | tf_op jit(solution)/shard_map/while/body/eval_jaxpr/dot_general | solution.py:25
  13.9 0.3 select_reduce_fusion.2
  14.3 3.8 %fusion.56 = f32[512,128]{1,0:T(8,128)S(1)} fusion(f32[1024]{0:T(1024)S(1)} %bitcast.56, s32[1024]{0:T(1024)S(1)} %bitcast.58, f32[2,1024,128]{2,1,0:T(8,128)S(1)} %get-tuple-element.448, s32[]{:T(128)} %get-tuple-element.435, f32[512,128]{1,0:T(8,128)S(1)} %get-tuple-element.436, pred[]{:T(512)S(6)} %compare.9), kind=kOutput, calls=%fused_computation.5.clone.1 | convolution fusion | flops 806486016 | bytes 1056773 | tf_op jit(solution)/shard_map/while/body/eval_jaxpr/dot_general | solution.py:25
  18.1 0.3 select_reduce_fusion.2
  18.5 0.7 copy-done
  19.2 0.0 reduce-scatter.4.cloned.1.call-update
  19.2 0.0 reduce-scatter.6.cloned.1.call-start
  19.2 0.6 convert_reduce_fusion
  19.8 42.2 %psum.50 = f32[]{:T(128)} all-reduce(f32[]{:T(128)} %convert_reduce_fusion), channel_id=1, replica_groups=mesh['grp'=4,'mem'=8] {'grp','mem'}, use_global_device_ids=true, to_apply=%region_9.10 | all-reduce | flops 1 | bytes 8 | tf_op jit(solution)/shard_map/psum | solution.py:83
  62.0 0.6 fusion.38
  63.2 13.0 %all-reduce.2 = f32[512]{0:T(512)S(1)} all-reduce(f32[512]{0:T(512)S(1)} %get-tuple-element.127), channel_id=2, replica_groups=mesh['grp'=4,'mem'=8] {'mem'}, use_global_device_ids=true, to_apply=%region_5.6.clone | all-reduce | flops 512 | bytes 4096
  76.2 0.1 dynamic-slice.3
  77.6 0.0 reduce-scatter.4.cloned.1.call-done
  77.6 18.8 %all-reduce.7 = (f32[64]{0:T(128)S(1)}, f32[64,128]{1,0:T(8,128)S(1)}) all-reduce(f32[64]{0:T(128)S(1)} %dynamic-slice.3, f32[64,128]{1,0:T(8,128)} %reduce-scatter.4.cloned.1.call-done), channel_id=1, replica_groups=mesh['grp'=4,'mem'=8] {'grp'}, use_global_device_ids=true, to_apply=%region_6.7 | all-reduce | flops 8256 | bytes 66048 | tf_op jit(solution)/shard_map/psum | solution.py:90
  96.4 0.1 broadcast_add_fusion.2
  96.5 0.1 slice_divide_fusion.2
  96.6 9.1 %all_gather.19 = f32[512,64]{1,0:T(8,128)S(1)} all-gather(f32[64,64]{1,0:T(8,128)S(1)} %get-tuple-element.274), channel_id=1, replica_groups=mesh['grp'=4,'mem'=8] {'mem'}, dimensions={0}, use_global_device_ids=true | all-gather | bytes 147456 | tf_op jit(solution)/shard_map/all_gather | solution.py:96
  105.7 8.5 %all_gather.20 = f32[512,64]{1,0:T(8,128)S(1)} all-gather(f32[64,64]{1,0:T(8,128)S(1)} %get-tuple-element.275), channel_id=1, replica_groups=mesh['grp'=4,'mem'=8] {'mem'}, dimensions={0}, use_global_device_ids=true | all-gather | bytes 147456 | tf_op jit(solution)/shard_map/all_gather | solution.py:97
  114.2 13.4 %all-reduce = f32[512]{0:T(512)S(1)} all-reduce(f32[512]{0:T(512)S(1)} %get-tuple-element.281), channel_id=1, replica_groups=mesh['grp'=4,'mem'=8] {'mem'}, use_global_device_ids=true, to_apply=%add | all-reduce | flops 512 | bytes 4096
  127.6 0.2 add_reduce_fusion.1
  127.8 0.1 pad_maximum_fusion.1
  127.9 12.2 %while.40 = (s32[]{:T(128)}, f32[512,128]{1,0:T(8,128)}, f32[512]{0:T(512)S(1)}, f32[512]{0:T(512)S(1)}, f32[2,1024,128]{2,1,0:T(8,128)S(1)}, /*index=5*/f32[512...) while((s32[]{:T(128)}, f32[512,128]{1,0:T(8,128)}, ...), condition=%wide.region_14.15_spmd.clone, body=%wide.region_10.14_spmd.clone.sunk | while | flops 1617559040 | bytes 10293372 | solution.py:39
  127.9 2.0 fusion.59
  130.0 0.3 fusion.60
  130.3 0.5 fusion.61
  130.8 2.7 convolution_add_fusion.4
  133.6 2.0 fusion.59
  135.6 0.3 fusion.60
  135.9 0.5 fusion.61
  136.5 3.7 %convolution_add_fusion.4 = f32[512,128]{1,0:T(8,128)} fusion(f32[2,1024,128]{2,1,0:T(8,128)S(1)} %get-tuple-element.475, s32[]{:T(128)} %get-tuple-element.461, f32[1024,512]{0,1:T(8,128)S(1)} %get-tuple-element.415, f32[1024]{0:T(1024)S(1)} %bitcast.52, f32[1024]{0:T(1024)S(1)} %fusion.60, f32[1024]{0:T(1024)S(1)} %get-tuple-element.416, ...), kind=kOutput, calls=%fused_computation.20.clone.1 | convolution fusion | flops 807010304 | bytes 3158021 | tf_op jit(solution)/shard_map/while/body/eval_jaxpr/dot_general | solution.py:25
  140.1 0.0 reduce-scatter.6.cloned.1.call-update
  140.1 0.0 reduce-scatter.8.cloned.1.call-start
  140.2 11.8 %all-reduce.3 = f32[512]{0:T(512)S(1)} all-reduce(f32[512]{0:T(512)S(1)} %get-tuple-element.129), channel_id=4, replica_groups=mesh['grp'=4,'mem'=8] {'mem'}, use_global_device_ids=true, to_apply=%region_17.18.clone | all-reduce | flops 512 | bytes 4096
  152.0 0.1 dynamic-slice.5
  152.1 19.0 %reduce-scatter.6.cloned.1.call-done = f32[64,128]{1,0:T(8,128)} async-done(((f32[512,128]{1,0:T(8,128)}), f32[64,128]{1,0:T(8,128)}) %reduce-scatter.6.cloned.1.call-update) | async-done | bytes 32784 | tf_op jit(solution)/shard_map/reduce_scatter | solution.py:87
  171.1 19.9 %all-reduce.6 = (f32[64]{0:T(128)S(1)}, f32[64,128]{1,0:T(8,128)S(1)}) all-reduce(f32[64]{0:T(128)S(1)} %dynamic-slice.5, f32[64,128]{1,0:T(8,128)} %reduce-scatter.6.cloned.1.call-done), channel_id=1, replica_groups=mesh['grp'=4,'mem'=8] {'grp'}, use_global_device_ids=true, to_apply=%region_18.19 | all-reduce | flops 8256 | bytes 66048 | tf_op jit(solution)/shard_map/psum | solution.py:90
  191.0 0.1 broadcast_add_fusion.1
  191.1 0.1 slice_divide_fusion.1
  191.2 9.3 %all_gather.22 = f32[512,64]{1,0:T(8,128)S(1)} all-gather(f32[64,64]{1,0:T(8,128)S(1)} %get-tuple-element.272), channel_id=1, replica_groups=mesh['grp'=4,'mem'=8] {'mem'}, dimensions={0}, use_global_device_ids=true | all-gather | bytes 147456 | tf_op jit(solution)/shard_map/all_gather | solution.py:96
  200.4 8.3 %all_gather.23 = f32[512,64]{1,0:T(8,128)S(1)} all-gather(f32[64,64]{1,0:T(8,128)S(1)} %get-tuple-element.273), channel_id=1, replica_groups=mesh['grp'=4,'mem'=8] {'mem'}, dimensions={0}, use_global_device_ids=true | all-gather | bytes 147456 | tf_op jit(solution)/shard_map/all_gather | solution.py:97
  208.8 13.4 %all-reduce.1 = f32[512]{0:T(512)S(1)} all-reduce(f32[512]{0:T(512)S(1)} %get-tuple-element.279), channel_id=1, replica_groups=mesh['grp'=4,'mem'=8] {'mem'}, use_global_device_ids=true, to_apply=%add.1 | all-reduce | flops 512 | bytes 4096
  222.2 0.2 add_reduce_fusion
  222.3 0.1 pad_maximum_fusion.2
  222.5 12.2 %while.41 = (s32[]{:T(128)}, f32[512,128]{1,0:T(8,128)}, f32[512]{0:T(512)S(1)}, f32[512]{0:T(512)S(1)}, f32[2,1024,128]{2,1,0:T(8,128)S(1)}, /*index=5*/f32[512...) while((s32[]{:T(128)}, f32[512,128]{1,0:T(8,128)}, ...), condition=%wide.region_24.25_spmd.clone, body=%wide.region_20.24_spmd.clone.sunk | while | flops 1617559040 | bytes 10293372 | solution.py:39
  222.5 2.0 fusion.64
  224.6 0.3 fusion.65
  224.9 0.5 fusion.66
  225.4 2.7 convolution_add_fusion.5
  228.2 2.0 fusion.64
  230.2 0.3 fusion.65
  230.5 0.5 fusion.66
  231.1 3.7 %convolution_add_fusion.5 = f32[512,128]{1,0:T(8,128)} fusion(f32[2,1024,128]{2,1,0:T(8,128)S(1)} %get-tuple-element.505, s32[]{:T(128)} %get-tuple-element.491, f32[1024,512]{0,1:T(8,128)S(1)} %get-tuple-element.425, f32[1024]{0:T(1024)S(1)} %bitcast.55, f32[1024]{0:T(1024)S(1)} %fusion.65, f32[1024]{0:T(1024)S(1)} %get-tuple-element.426, ...), kind=kOutput, calls=%fused_computation.35.clone.1 | convolution fusion | flops 807010304 | bytes 3158021 | tf_op jit(solution)/shard_map/while/body/eval_jaxpr/dot_general | solution.py:25
  234.7 0.0 reduce-scatter.8.cloned.1.call-update
  234.7 11.8 %all-reduce.4 = f32[512]{0:T(512)S(1)} all-reduce(f32[512]{0:T(512)S(1)} %get-tuple-element.132), channel_id=7, replica_groups=mesh['grp'=4,'mem'=8] {'mem'}, use_global_device_ids=true, to_apply=%region_27.28.clone | all-reduce | flops 512 | bytes 4096
  246.5 0.1 dynamic-slice.7
  246.6 19.2 %reduce-scatter.8.cloned.1.call-done = f32[64,128]{1,0:T(8,128)} async-done(((f32[512,128]{1,0:T(8,128)}), f32[64,128]{1,0:T(8,128)}) %reduce-scatter.8.cloned.1.call-update) | async-done | bytes 32784 | tf_op jit(solution)/shard_map/reduce_scatter | solution.py:87
  265.8 19.9 %all-reduce.5 = (f32[64,128]{1,0:T(8,128)S(1)}, f32[64]{0:T(128)S(1)}) all-reduce(f32[64,128]{1,0:T(8,128)} %reduce-scatter.8.cloned.1.call-done, f32[64]{0:T(128)S(1)} %dynamic-slice.7), channel_id=1, replica_groups=mesh['grp'=4,'mem'=8] {'grp'}, use_global_device_ids=true, to_apply=%region_26.27 | all-reduce | flops 8256 | bytes 66048 | tf_op jit(solution)/shard_map/psum | solution.py:90
  285.7 0.5 broadcast_divide_fusion.2
  286.2 0.7 fusion.31
  (37 shorter events, 0.2 us)
Async XLA Ops:
  7.2 70.4 %reduce-scatter.4.cloned.1.call-start = ((), (), s32[]{:S(2)}) async-start(), calls=%async_computation.3 | async-start | bytes 294912 | tf_op jit(solution)/shard_map/reduce_scatter | solution.py:87
  8.5 1.5 copy-start.2
  8.5 1.5 copy-start.1
  10.1 51.9 %copy-start.3 = (u32[32]{0:T(128)S(1)}, u32[32]{0:T(128)}, u32[]{:S(2)}) copy-start(u32[32]{0:T(128)} %constant.58) | copy-start | bytes 388
  18.5 0.7 copy-start
  19.2 151.9 %reduce-scatter.6.cloned.1.call-start = ((), (), s32[]{:S(2)}) async-start(), calls=%async_computation.4 | async-start | bytes 294912 | tf_op jit(solution)/shard_map/reduce_scatter | solution.py:87
  140.1 125.7 %reduce-scatter.8.cloned.1.call-start = ((), (), s32[]{:S(2)}) async-start(), calls=%async_computation.5 | async-start | bytes 294912 | tf_op jit(solution)/shard_map/reduce_scatter | solution.py:87
Sparse Core Ops, SparseCore 0:
  19.3 36.3 reduce-scatter.3
  140.3 30.7 reduce-scatter.5
  234.9 30.9 reduce-scatter.7
where the time goes:
time: 294 us; the launch traced here: 293 us
  blocking collectives  199 us (68%)
  waiting for transfers between devices  38.3 us (13%)
  matrix products  28.4 us (10%)
  between operations  15.9 us (5%)
  other arithmetic  9.37 us (3%)
    unnamed x5, blocking collectives  63.3 us
    psum x3, blocking collectives, combine(): return lax.psum((shared[0], shared[1]), 'grp')  58.5 us
    psum x1, blocking collectives, shards(): total = lax.psum(jnp.sum(virtual), ('grp', 'mem'))  42.2 us
    reduce_scatter x3, waiting for transfers between devices, combine(): lax.psum_scatter(local_sums, 'mem', scatter_dimension=0, tiled=True)  38.2 us
    dot_general x6, matrix products, advance(): lax.dot_general(weights, piece[0], (((0,), (0,)), ((), ())), precision=la...  20.3 us
    all_gather x2, blocking collectives, shards(): lax.all_gather(means, 'mem', axis=0, tiled=True)  18.4 us
    all_gather x2, blocking collectives, shards(): lax.all_gather(variances, 'mem', axis=0, tiled=True)  16.8 us
    dot_general x4, matrix products, soft_weights(): lax.dot_general(block_features, table, (((1,), (1,)), ((), ())), precisio...  8.14 us
  transfers between devices with their start and end apart: 3, of which 2 were waited for; matrix products, arithmetic and copies ran while one was open for 0% of the time, Pallas kernels for 0%

commit v1 on v0

--- a/solution.py
+++ b/solution.py
@@ -6,6 +6,19 @@
 
 P_SIZE = 512
 ITERS = 2
+
+
+def collect(x, axis, dim):
+    ways = lax.axis_size(axis)
+    up = [(d, (d + 1) % ways) for d in range(ways)]
+    down = [(d, (d - 1) % ways) for d in range(ways)]
+    earlier, later = ([x], [x])
+    for _ in range(ways // 2):
+        earlier.append(lax.ppermute(earlier[-1], axis, up))
+    for _ in range((ways - 1) // 2):
+        later.append(lax.ppermute(later[-1], axis, down))
+    line = jnp.concatenate([*earlier[::-1], *later[1:]], axis=dim)
+    return jnp.roll(line, (lax.axis_index(axis) - ways // 2) * x.shape[dim], axis=dim)
 
 
 def child_features(means, variances):
@@ -94,7 +107,7 @@
     for iteration in range(ITERS):
         all_means, all_variances, all_weights = (
             lax.all_gather(means, "mem", axis=0, tiled=True),
-            lax.all_gather(variances, "mem", axis=0, tiled=True),
+            collect(variances, "mem", 0),
             lax.all_gather(weights, "mem", axis=0, tiled=True),
         )
         table, offset, log_weight = parent_table(all_means, all_variances, all_weights)

time: 294 us -> 307 us (1.044)
  waiting for transfers between devices: 38.3 us -> 50.7 us
  starting transfers between devices: 0.12 us -> 9.94 us
  blocking collectives: 199 us -> 190 us
    all_gather x2 -> x0, blocking collectives: 16.8 us -> none  [shards(): lax.all_gather(variances, 'mem', axis=0, tiled=True)]
    ppermute x0 -> x14, waiting for transfers between devices: none -> 15 us  [the longest x8 11.9 us: collect(): earlier.append(lax.ppermute(earlier[-1], axis, up))]
    ppermute x0 -> x14, starting transfers between devices: none -> 9.82 us  [the longest x6 8.72 us: collect(): later.append(lax.ppermute(later[-1], axis, down))]
    unnamed x5, blocking collectives: 63.3 us -> 70.6 us
  transfers between devices with their start and end apart: 3 -> 17, of which waited for: 2 -> 8; matrix products, arithmetic and copies ran while one was open for 0% -> 0% of each run, Pallas kernels for 0% -> 0%
where the time goes in v1:
time: 307 us; the launch traced here: 306 us
  blocking collectives  190 us (62%)
  waiting for transfers between devices  50.7 us (17%)
  matrix products  28.4 us (9%)
  between operations  16 us (5%)
  starting transfers between devices  9.94 us (3%)
  other arithmetic  9.59 us (3%)
    unnamed x5, blocking collectives  70.6 us
    psum x3, blocking collectives, combine(): return lax.psum((shared[0], shared[1]), 'grp')  58.4 us
    psum x1, blocking collectives, shards(): total = lax.psum(jnp.sum(virtual), ('grp', 'mem'))  42.2 us
    reduce_scatter x3, waiting for transfers between devices, combine(): lax.psum_scatter(local_sums, 'mem', scatter_dimension=0, tiled=True)  35.6 us
    dot_general x6, matrix products, advance(): lax.dot_general(weights, piece[0], (((0,), (0,)), ((), ())), precision=la...  20.3 us
    all_gather x2, blocking collectives, shards(): lax.all_gather(means, 'mem', axis=0, tiled=True)  18.4 us
    ppermute x8, waiting for transfers between devices, collect(): earlier.append(lax.ppermute(earlier[-1], axis, up))  11.9 us
    ppermute x6, starting transfers between devices, collect(): later.append(lax.ppermute(later[-1], axis, down))  8.72 us
  transfers between devices with their start and end apart: 17, of which 8 were waited for; matrix products, arithmetic and copies ran while one was open for 0% of the time, Pallas kernels for 0%

profile of v1, /device:TPU:0, one launch (start us, length us, event | category | flops | bytes accessed | tf_op | source)
XLA Modules:
  0.0 306.5 jit_solution(6520299033157806422)
XLA Ops:
  7.2 1.3 multiply_add_fusion.2
  8.5 1.2 pad_maximum_fusion
  9.7 0.3 copy.9
  10.1 8.4 %while.39 = (s32[]{:T(128)}, f32[512,128]{1,0:T(8,128)S(1)}, f32[512]{0:T(512)S(1)}, s32[2,1024,1]{1,2,0:T(1,128)S(1)}, f32[2,1024]{1,0:T(2,128)S(1)}, /*index=5*/f32[2,1024,128]{2,1,0:T(8,128)S(1)}, s32[]{:T(128)}, s32[]{:T(128)}) while((s32[]{:T(128)}, f32[512,128]{1,0:T(8,128)S(1)}, f32[512]{0:T(512)S(1)}, ...), condition=%wide.region_2.3_spmd.clone, body=%wide.region_0.2_spmd.clone.sunk | while | flops 808059392 | bytes 1089644 | solution.py:52
  10.1 3.8 %fusion.58 = f32[512,128]{1,0:T(8,128)S(1)} fusion(f32[1024]{0:T(1024)S(1)} %bitcast.56, s32[1024]{0:T(1024)S(1)} %bitcast.58, f32[2,1024,128]{2,1,0:T(8,128)S(1)} %get-tuple-element.447, s32[]{:T(128)} %get-tuple-element.434, f32[512,128]{1,0:T(8,128)S(1)} %get-tuple-element.435, pred[]{:T(512)S(6)} %compare.10), kind=kOutput, calls=%fused_computation.5.clone.1 | convolution fusion | flops 806486016 | bytes 1056773 | tf_op jit(solution)/shard_map/while/body/eval_jaxpr/dot_general | solution.py:38
  13.9 0.3 select_reduce_fusion.2
  14.3 3.8 %fusion.58 = f32[512,128]{1,0:T(8,128)S(1)} fusion(f32[1024]{0:T(1024)S(1)} %bitcast.56, s32[1024]{0:T(1024)S(1)} %bitcast.58, f32[2,1024,128]{2,1,0:T(8,128)S(1)} %get-tuple-element.447, s32[]{:T(128)} %get-tuple-element.434, f32[512,128]{1,0:T(8,128)S(1)} %get-tuple-element.435, pred[]{:T(512)S(6)} %compare.10), kind=kOutput, calls=%fused_computation.5.clone.1 | convolution fusion | flops 806486016 | bytes 1056773 | tf_op jit(solution)/shard_map/while/body/eval_jaxpr/dot_general | solution.py:38
  18.1 0.3 select_reduce_fusion.2
  18.5 0.7 copy-done
  19.2 0.6 convert_reduce_fusion
  19.8 42.2 %psum.50 = f32[]{:T(128)} all-reduce(f32[]{:T(128)} %convert_reduce_fusion), channel_id=1, replica_groups=mesh['grp'=4,'mem'=8] {'grp','mem'}, use_global_device_ids=true, to_apply=%region_9.11 | all-reduce | flops 1 | bytes 8 | tf_op jit(solution)/shard_map/psum | solution.py:96
  62.0 0.6 fusion.40
  63.2 12.9 %all-reduce.2 = f32[512]{0:T(512)S(1)} all-reduce(f32[512]{0:T(512)S(1)} %get-tuple-element.128), channel_id=2, replica_groups=mesh['grp'=4,'mem'=8] {'mem'}, use_global_device_ids=true, to_apply=%region_5.6.clone | all-reduce | flops 512 | bytes 4096
  77.5 18.7 %all-reduce.7 = (f32[64]{0:T(128)S(1)}, f32[64,128]{1,0:T(8,128)S(1)}) all-reduce(f32[64]{0:T(128)S(1)} %dynamic-slice.3, f32[64,128]{1,0:T(8,128)} %reduce-scatter.4.cloned.1.call-done), channel_id=1, replica_groups=mesh['grp'=4,'mem'=8] {'grp'}, use_global_device_ids=true, to_apply=%region_6.7 | all-reduce | flops 8256 | bytes 66048 | tf_op jit(solution)/shard_map/psum | solution.py:103
  96.3 0.1 broadcast_add_fusion.2
  96.4 0.1 fusion.37
  96.5 4.2 %collective-permute-done = f32[64,64]{1,0:T(8,128)S(1)} collective-permute-done((f32[64,64]{1,0:T(8,128)S(1)}, f32[64,64]{1,0:T(8,128)S(1)}, u32[]{:S(2)}, u32[]{:S(2)}) %collective-permute-start) | collective-permute-done | bytes 16416 | tf_op jit(solution)/shard_map/ppermute | solution.py:17
  100.8 2.6 collective-permute-start.4
  103.4 1.6 collective-permute-done.1
  105.0 14.4 %all-reduce = f32[512]{0:T(512)S(1)} all-reduce(f32[512]{0:T(512)S(1)} %get-tuple-element.280), channel_id=1, replica_groups=mesh['grp'=4,'mem'=8] {'mem'}, use_global_device_ids=true, to_apply=%add | all-reduce | flops 512 | bytes 4096
  119.5 0.5 collective-permute-start.3
  120.0 9.2 %all_gather.13 = f32[512,64]{1,0:T(8,128)S(1)} all-gather(f32[64,64]{1,0:T(8,128)S(1)} %get-tuple-element.274), channel_id=1, replica_groups=mesh['grp'=4,'mem'=8] {'mem'}, dimensions={0}, use_global_device_ids=true | all-gather | bytes 147456 | tf_op jit(solution)/shard_map/all_gather | solution.py:109
  129.2 1.6 collective-permute-start.6
  130.9 1.5 collective-permute-done.6
  132.4 0.3 add_reduce_fusion.1
  132.7 0.1 pad_maximum_fusion.1
  132.8 12.2 %while.40 = (s32[]{:T(128)}, f32[512,128]{1,0:T(8,128)}, f32[512]{0:T(512)S(1)}, f32[512]{0:T(512)S(1)}, f32[2,1024,128]{2,1,0:T(8,128)S(1)}, /*index=5*/f32[512...) while((s32[]{:T(128)}, f32[512,128]{1,0:T(8,128)}, ...), condition=%wide.region_14.16_spmd.clone, body=%wide.region_10.15_spmd.clone.sunk | while | flops 1617559040 | bytes 10293372 | solution.py:52
  132.9 2.0 fusion.61
  134.9 0.3 fusion.62
  135.3 0.5 fusion.63
  135.8 2.7 convolution_add_fusion.4
  138.5 2.0 fusion.61
  140.6 0.3 fusion.62
  140.9 0.5 fusion.63
  141.4 3.7 %convolution_add_fusion.4 = f32[512,128]{1,0:T(8,128)} fusion(f32[2,1024,128]{2,1,0:T(8,128)S(1)} %get-tuple-element.474, s32[]{:T(128)} %get-tuple-element.460, f32[1024,512]{0,1:T(8,128)S(1)} %get-tuple-element.414, f32[1024]{0:T(1024)S(1)} %bitcast.52, f32[1024]{0:T(1024)S(1)} %fusion.62, f32[1024]{0:T(1024)S(1)} %get-tuple-element.415, ...), kind=kOutput, calls=%fused_computation.20.clone.1 | convolution fusion | flops 807010304 | bytes 3158021 | tf_op jit(solution)/shard_map/while/body/eval_jaxpr/dot_general | solution.py:38
  145.2 14.4 %all-reduce.3 = f32[512]{0:T(512)S(1)} all-reduce(f32[512]{0:T(512)S(1)} %get-tuple-element.130), channel_id=4, replica_groups=mesh['grp'=4,'mem'=8] {'mem'}, use_global_device_ids=true, to_apply=%region_17.19.clone | all-reduce | flops 512 | bytes 4096
  159.7 17.8 %reduce-scatter.6.cloned.1.call-done = f32[64,128]{1,0:T(8,128)} async-done(((f32[512,128]{1,0:T(8,128)}), f32[64,128]{1,0:T(8,128)}) %reduce-scatter.6.cloned.1.call-update) | async-done | bytes 32784 | tf_op jit(solution)/shard_map/reduce_scatter | solution.py:100
  177.4 19.8 %all-reduce.6 = (f32[64]{0:T(128)S(1)}, f32[64,128]{1,0:T(8,128)S(1)}) all-reduce(f32[64]{0:T(128)S(1)} %dynamic-slice.5, f32[64,128]{1,0:T(8,128)} %reduce-scatter.6.cloned.1.call-done), channel_id=1, replica_groups=mesh['grp'=4,'mem'=8] {'grp'}, use_global_device_ids=true, to_apply=%region_18.20 | all-reduce | flops 8256 | bytes 66048 | tf_op jit(solution)/shard_map/psum | solution.py:103
  197.3 0.1 broadcast_add_fusion.1
  197.4 0.1 fusion.35
  197.6 4.2 %collective-permute-done.7 = f32[64,64]{1,0:T(8,128)S(1)} collective-permute-done((f32[64,64]{1,0:T(8,128)S(1)}, f32[64,64]{1,0:T(8,128)S(1)}, u32[]{:S(2)}, u32[]{:S(2)}) %collective-permute-start.7) | collective-permute-done | bytes 16416 | tf_op jit(solution)/shard_map/ppermute | solution.py:17
  201.8 2.6 collective-permute-start.11
  204.4 1.9 collective-permute-done.8
  206.3 14.4 %all-reduce.1 = f32[512]{0:T(512)S(1)} all-reduce(f32[512]{0:T(512)S(1)} %get-tuple-element.278), channel_id=1, replica_groups=mesh['grp'=4,'mem'=8] {'mem'}, use_global_device_ids=true, to_apply=%add.1 | all-reduce | flops 512 | bytes 4096
  220.8 0.5 collective-permute-start.10
  221.3 9.3 %all_gather.15 = f32[512,64]{1,0:T(8,128)S(1)} all-gather(f32[64,64]{1,0:T(8,128)S(1)} %get-tuple-element.272), channel_id=1, replica_groups=mesh['grp'=4,'mem'=8] {'mem'}, dimensions={0}, use_global_device_ids=true | all-gather | bytes 147456 | tf_op jit(solution)/shard_map/all_gather | solution.py:109
  230.6 1.7 collective-permute-start.13
  232.3 1.5 collective-permute-done.13
  233.9 0.3 add_reduce_fusion
  234.2 0.1 pad_maximum_fusion.2
  234.3 12.2 %while.41 = (s32[]{:T(128)}, f32[512,128]{1,0:T(8,128)}, f32[512]{0:T(512)S(1)}, f32[512]{0:T(512)S(1)}, f32[2,1024,128]{2,1,0:T(8,128)S(1)}, /*index=5*/f32[512...) while((s32[]{:T(128)}, f32[512,128]{1,0:T(8,128)}, ...), condition=%wide.region_24.26_spmd.clone, body=%wide.region_20.25_spmd.clone.sunk | while | flops 1617559040 | bytes 10293372 | solution.py:52
  234.3 2.0 fusion.66
  236.4 0.3 fusion.67
  236.7 0.5 fusion.68
  237.2 2.7 convolution_add_fusion.5
  240.0 2.0 fusion.66
  242.0 0.3 fusion.67
  242.4 0.5 fusion.68
  242.9 3.7 %convolution_add_fusion.5 = f32[512,128]{1,0:T(8,128)} fusion(f32[2,1024,128]{2,1,0:T(8,128)S(1)} %get-tuple-element.504, s32[]{:T(128)} %get-tuple-element.490, f32[1024,512]{0,1:T(8,128)S(1)} %get-tuple-element.424, f32[1024]{0:T(1024)S(1)} %bitcast.55, f32[1024]{0:T(1024)S(1)} %fusion.67, f32[1024]{0:T(1024)S(1)} %get-tuple-element.425, ...), kind=kOutput, calls=%fused_computation.35.clone.1 | convolution fusion | flops 807010304 | bytes 3158021 | tf_op jit(solution)/shard_map/while/body/eval_jaxpr/dot_general | solution.py:38
  246.6 14.4 %all-reduce.4 = f32[512]{0:T(512)S(1)} all-reduce(f32[512]{0:T(512)S(1)} %get-tuple-element.133), channel_id=7, replica_groups=mesh['grp'=4,'mem'=8] {'mem'}, use_global_device_ids=true, to_apply=%region_27.29.clone | all-reduce | flops 512 | bytes 4096
  261.1 17.8 %reduce-scatter.8.cloned.1.call-done = f32[64,128]{1,0:T(8,128)} async-done(((f32[512,128]{1,0:T(8,128)}), f32[64,128]{1,0:T(8,128)}) %reduce-scatter.8.cloned.1.call-update) | async-done | bytes 32784 | tf_op jit(solution)/shard_map/reduce_scatter | solution.py:100
  278.9 19.8 %all-reduce.5 = (f32[64,128]{1,0:T(8,128)S(1)}, f32[64]{0:T(128)S(1)}) all-reduce(f32[64,128]{1,0:T(8,128)} %reduce-scatter.8.cloned.1.call-done, f32[64]{0:T(128)S(1)} %dynamic-slice.7), channel_id=1, replica_groups=mesh['grp'=4,'mem'=8] {'grp'}, use_global_device_ids=true, to_apply=%region_26.28 | all-reduce | flops 8256 | bytes 66048 | tf_op jit(solution)/shard_map/psum | solution.py:103
  298.7 0.5 broadcast_divide_fusion.2
  299.2 0.7 fusion.33
  (81 shorter events, 1.0 us)
Async XLA Ops:
  7.2 70.4 %reduce-scatter.4.cloned.1.call-start = ((), (), s32[]{:S(2)}) async-start(), calls=%async_computation.3 | async-start | bytes 294912 | tf_op jit(solution)/shard_map/reduce_scatter | solution.py:100
  8.5 1.5 copy-start.2
  8.5 1.6 copy-start.1
  10.1 51.9 %copy-start.3 = (u32[32]{0:T(128)S(1)}, u32[32]{0:T(128)}, u32[]{:S(2)}) copy-start(u32[32]{0:T(128)} %constant.84) | copy-start | bytes 388
  18.5 0.7 copy-start
  19.2 158.3 %reduce-scatter.6.cloned.1.call-start = ((), (), s32[]{:S(2)}) async-start(), calls=%async_computation.4 | async-start | bytes 294912 | tf_op jit(solution)/shard_map/reduce_scatter | solution.py:100
  96.5 4.3 %collective-permute-start = (f32[64,64]{1,0:T(8,128)S(1)}, f32[64,64]{1,0:T(8,128)S(1)}, u32[]{:S(2)}, u32[]{:S(2)}) collective-permute-start(f32[64,64]{1,0:T(8,128)S(1)} %get-tuple-element.273), channel_id=1, source_target_pairs={{0,1},{1,2},{2,3},{3,4},{4,5},{5,6},{6,7},{7,0},{8,9},{9,10},{10,1... | collective-permute-start | bytes 49160 | tf_op jit(solution)/shard_map/ppermute | solution.py:17
  100.8 4.2 %collective-permute-start.1 = (f32[64,64]{1,0:T(8,128)S(1)}, f32[64,64]{1,0:T(8,128)S(1)}, u32[]{:S(2)}, u32[]{:S(2)}) collective-permute-start(f32[64,64]{1,0:T(8,128)S(1)} %collective-permute-done), channel_id=1, source_target_pairs={{0,1},{1,2},{2,3},{3,4},{4,5},{5,6},{6,7},{7,0},{8,9},{9,10},{10,1... | collective-permute-start | bytes 49160 | tf_op jit(solution)/shard_map/ppermute | solution.py:17
  100.8 18.7 %collective-permute-start.4 = (f32[64,64]{1,0:T(8,128)S(1)}, f32[64,64]{1,0:T(8,128)S(1)}, u32[]{:S(2)}, u32[]{:S(2)}) collective-permute-start(f32[64,64]{1,0:T(8,128)S(1)} %get-tuple-element.273), channel_id=1, source_target_pairs={{0,7},{1,0},{2,1},{3,2},{4,3},{5,4},{6,5},{7,6},{8,15},{9,8},{10,9... | collective-permute-start | bytes 49160 | tf_op jit(solution)/shard_map/ppermute | solution.py:19
  105.0 14.5 %collective-permute-start.2 = (f32[64,64]{1,0:T(8,128)S(1)}, f32[64,64]{1,0:T(8,128)S(1)}, u32[]{:S(2)}, u32[]{:S(2)}) collective-permute-start(f32[64,64]{1,0:T(8,128)S(1)} %collective-permute-done.1), channel_id=1, source_target_pairs={{0,1},{1,2},{2,3},{3,4},{4,5},{5,6},{6,7},{7,0},{8,9},{9,10},{10,1... | collective-permute-start | bytes 49160 | tf_op jit(solution)/shard_map/ppermute | solution.py:17
  119.4 9.7 %collective-permute-start.5 = (f32[64,64]{1,0:T(8,128)S(1)}, f32[64,64]{1,0:T(8,128)S(1)}, u32[]{:S(2)}, u32[]{:S(2)}) collective-permute-start(f32[64,64]{1,0:T(8,128)S(1)} %collective-permute-done.4), channel_id=1, source_target_pairs={{0,7},{1,0},{2,1},{3,2},{4,3},{5,4},{6,5},{7,6},{8,15},{9,8},{10,9... | collective-permute-start | bytes 49160 | tf_op jit(solution)/shard_map/ppermute | solution.py:19
  119.5 11.3 %collective-permute-start.3 = (f32[64,64]{1,0:T(8,128)S(1)}, f32[64,64]{1,0:T(8,128)S(1)}, u32[]{:S(2)}, u32[]{:S(2)}) collective-permute-start(f32[64,64]{1,0:T(8,128)S(1)} %collective-permute-done.2), channel_id=1, source_target_pairs={{0,1},{1,2},{2,3},{3,4},{4,5},{5,6},{6,7},{7,0},{8,9},{9,10},{10,1... | collective-permute-start | bytes 49160 | tf_op jit(solution)/shard_map/ppermute | solution.py:17
  129.2 3.2 %collective-permute-start.6 = (f32[64,64]{1,0:T(8,128)S(1)}, f32[64,64]{1,0:T(8,128)S(1)}, u32[]{:S(2)}, u32[]{:S(2)}) collective-permute-start(f32[64,64]{1,0:T(8,128)S(1)} %collective-permute-done.5), channel_id=1, source_target_pairs={{0,7},{1,0},{2,1},{3,2},{4,3},{5,4},{6,5},{7,6},{8,15},{9,8},{10,9... | collective-permute-start | bytes 49160 | tf_op jit(solution)/shard_map/ppermute | solution.py:19
  145.1 133.8 %reduce-scatter.8.cloned.1.call-start = ((), (), s32[]{:S(2)}) async-start(), calls=%async_computation.5 | async-start | bytes 294912 | tf_op jit(solution)/shard_map/reduce_scatter | solution.py:100
  197.5 4.3 %collective-permute-start.7 = (f32[64,64]{1,0:T(8,128)S(1)}, f32[64,64]{1,0:T(8,128)S(1)}, u32[]{:S(2)}, u32[]{:S(2)}) collective-permute-start(f32[64,64]{1,0:T(8,128)S(1)} %get-tuple-element.271), channel_id=1, source_target_pairs={{0,1},{1,2},{2,3},{3,4},{4,5},{5,6},{6,7},{7,0},{8,9},{9,10},{10,1... | collective-permute-start | bytes 49160 | tf_op jit(solution)/shard_map/ppermute | solution.py:17
  201.8 4.5 %collective-permute-start.8 = (f32[64,64]{1,0:T(8,128)S(1)}, f32[64,64]{1,0:T(8,128)S(1)}, u32[]{:S(2)}, u32[]{:S(2)}) collective-permute-start(f32[64,64]{1,0:T(8,128)S(1)} %collective-permute-done.7), channel_id=1, source_target_pairs={{0,1},{1,2},{2,3},{3,4},{4,5},{5,6},{6,7},{7,0},{8,9},{9,10},{10,1... | collective-permute-start | bytes 49160 | tf_op jit(solution)/shard_map/ppermute | solution.py:17
  201.8 19.0 %collective-permute-start.11 = (f32[64,64]{1,0:T(8,128)S(1)}, f32[64,64]{1,0:T(8,128)S(1)}, u32[]{:S(2)}, u32[]{:S(2)}) collective-permute-start(f32[64,64]{1,0:T(8,128)S(1)} %get-tuple-element.271), channel_id=1, source_target_pairs={{0,7},{1,0},{2,1},{3,2},{4,3},{5,4},{6,5},{7,6},{8,15},{9,8},{10,9... | collective-permute-start | bytes 49160 | tf_op jit(solution)/shard_map/ppermute | solution.py:19
  206.3 14.5 %collective-permute-start.9 = (f32[64,64]{1,0:T(8,128)S(1)}, f32[64,64]{1,0:T(8,128)S(1)}, u32[]{:S(2)}, u32[]{:S(2)}) collective-permute-start(f32[64,64]{1,0:T(8,128)S(1)} %collective-permute-done.8), channel_id=1, source_target_pairs={{0,1},{1,2},{2,3},{3,4},{4,5},{5,6},{6,7},{7,0},{8,9},{9,10},{10,1... | collective-permute-start | bytes 49160 | tf_op jit(solution)/shard_map/ppermute | solution.py:17
  220.8 9.8 %collective-permute-start.12 = (f32[64,64]{1,0:T(8,128)S(1)}, f32[64,64]{1,0:T(8,128)S(1)}, u32[]{:S(2)}, u32[]{:S(2)}) collective-permute-start(f32[64,64]{1,0:T(8,128)S(1)} %collective-permute-done.11), channel_id=1, source_target_pairs={{0,7},{1,0},{2,1},{3,2},{4,3},{5,4},{6,5},{7,6},{8,15},{9,8},{10,9... | collective-permute-start | bytes 49160 | tf_op jit(solution)/shard_map/ppermute | solution.py:19
  220.8 11.4 %collective-permute-start.10 = (f32[64,64]{1,0:T(8,128)S(1)}, f32[64,64]{1,0:T(8,128)S(1)}, u32[]{:S(2)}, u32[]{:S(2)}) collective-permute-start(f32[64,64]{1,0:T(8,128)S(1)} %collective-permute-done.9), channel_id=1, source_target_pairs={{0,1},{1,2},{2,3},{3,4},{4,5},{5,6},{6,7},{7,0},{8,9},{9,10},{10,1... | collective-permute-start | bytes 49160 | tf_op jit(solution)/shard_map/ppermute | solution.py:17
  230.6 3.3 %collective-permute-start.13 = (f32[64,64]{1,0:T(8,128)S(1)}, f32[64,64]{1,0:T(8,128)S(1)}, u32[]{:S(2)}, u32[]{:S(2)}) collective-permute-start(f32[64,64]{1,0:T(8,128)S(1)} %collective-permute-done.12), channel_id=1, source_target_pairs={{0,7},{1,0},{2,1},{3,2},{4,3},{5,4},{6,5},{7,6},{8,15},{9,8},{10,9... | collective-permute-start | bytes 49160 | tf_op jit(solution)/shard_map/ppermute | solution.py:19
Sparse Core Ops, SparseCore 0:
  19.3 36.3 reduce-scatter.3
  145.2 32.1 reduce-scatter.5
  246.7 32.1 reduce-scatter.7
